TPU v7x, 512 devices: a whole 4x8x8 slice. The times are simulated.
512 devices in a mesh: dp: 32 (over x, y), segment: 2 (over core), mp: 8 (over z).
Axes of the slice: x: 4, y: 8, z: 8, core: 2. Of those that a mesh axis runs over, the one named last changes fastest.
Arguments:
- frames: bfloat16 [2, 8192, 1280], P(None, ('dp', 'mp')), may hold values from -8 to 8
- dec_states: bfloat16 [2, 2048, 1280], P(None, 'dp'), may hold values from -8 to 8
- out_grad: bfloat16 [2, 2048, 1280], P(None, 'dp'), may hold values from -3 to 3
- frame_lengths: int32 [2, 32, 4], P(None, 'dp'), may hold values from 1 to 128, 256 in all within a row
- token_lengths: int32 [2, 32, 4], P(None, 'dp'), may hold values from 1 to 32, 64 in all within a row
- weights: bfloat16 [2, 4, 1024, 1280], P('segment', None, 'mp'), may hold values from -1 to 1
- norm_gains: float32 [3, 1280], replicated, may hold values from 0.25 to 1.75
- norm_biases: float32 [3, 1280], replicated, may hold values from -2 to 2
Outputs:
- gradient: float32 [2, 3, 1024, 1280], P('segment', None, 'mp')
Inputs may be any that keep to these rules, and one draw needn't show every extreme that they name: `frame_lengths`: the 4 utterance lengths of each micro-batch and group sum to 256. `token_lengths`: the 4 token counts of each micro-batch and group sum to 64.
All inputs are finite; a program needn't handle non-finite values.
Results may differ from a plain program's by a relative error of at most 0.04.
Values may be sent and summed in bfloat16 or wider, within the bound.
No kernel may reach another device: no remote copies, remote signals or barrier semaphores. Data moves between devices by JAX's collectives and lax.ppermute only.
A program may use at most 64 MiB of HBM per device.

v0:
```python
import math
import jax
import jax.numpy as jnp
from jax import lax
from jax.sharding import PartitionSpec as P

HS = 64
EPSILON = 1e-05
ROWS_DIMS = (((0,), (0,)), ((), ()))
FEAT_DIMS = (((1,), (1,)), ((), ()))


def layer_norm(values, norm_gain, offset):
    center = values - jnp.mean(values, axis=-1, keepdims=True)
    variance = jnp.mean(center * center, axis=-1, keepdims=True)
    return center * lax.rsqrt(variance + EPSILON) * norm_gain + offset


def norm_backward(grad_out, values, norm_gain):
    center = values - jnp.mean(values, axis=-1, keepdims=True)
    variance = jnp.mean(center * center, axis=-1, keepdims=True)
    inverse = lax.rsqrt(variance + EPSILON)
    normed = center * inverse
    scaled = grad_out * norm_gain
    return inverse * (
        scaled
        - jnp.mean(scaled, axis=-1, keepdims=True)
        - normed * jnp.mean(scaled * normed, axis=-1, keepdims=True)
    )


def utterance_ids(lengths, row_count):
    bounds = jnp.cumsum(lengths, dtype=jnp.int32)
    places = jnp.arange(row_count, dtype=jnp.int32)
    return jnp.sum((places[:, None] >= bounds[None, :]).astype(jnp.int32), axis=1)


def project(row_block, matrix):
    return lax.dot_general(row_block, matrix, FEAT_DIMS, preferred_element_type=jnp.float32).astype(
        jnp.bfloat16
    )


def outer_rows(left_rows, right_rows):
    return lax.dot_general(left_rows, right_rows, ROWS_DIMS, preferred_element_type=jnp.float32)


def split_heads(row_block):
    return row_block.reshape(row_block.shape[0], -1, HS)


def attend(queries, key_rows, value_rows, allowed):
    scaling = 1.0 / math.sqrt(HS)
    scores = (
        jnp.einsum(
            "qhd,khd->hqk",
            split_heads(queries),
            split_heads(key_rows),
            preferred_element_type=jnp.float32,
        )
        * scaling
    )
    scores = jnp.where(allowed[None], scores, -1e30)
    highest = jnp.max(scores, axis=-1, keepdims=True)
    raised = jnp.exp(scores - highest)
    attn_probs = raised / jnp.sum(raised, axis=-1, keepdims=True)
    context = jnp.einsum(
        "hqk,khd->qhd",
        attn_probs.astype(jnp.bfloat16),
        split_heads(value_rows),
        preferred_element_type=jnp.float32,
    )
    return (context.reshape(queries.shape[0], -1).astype(jnp.bfloat16), attn_probs)


def attend_backward(queries, key_rows, value_rows, attn_probs, grad_context):
    scaling = 1.0 / math.sqrt(HS)
    grad_heads = split_heads(grad_context)
    grad_probs = jnp.einsum(
        "qhd,khd->hqk", grad_heads, split_heads(value_rows), preferred_element_type=jnp.float32
    )
    grad_scores = (
        attn_probs * (grad_probs - jnp.sum(grad_probs * attn_probs, axis=-1, keepdims=True))
    ).astype(jnp.bfloat16)
    key_grad = (
        jnp.einsum(
            "hqk,qhd->khd", grad_scores, split_heads(queries), preferred_element_type=jnp.float32
        )
        * scaling
    )
    key_grad = key_grad.reshape(key_rows.shape[0], -1).astype(jnp.bfloat16)
    value_grad = jnp.einsum(
        "hqk,qhd->khd",
        attn_probs.astype(jnp.bfloat16),
        grad_heads,
        preferred_element_type=jnp.float32,
    )
    value_grad = value_grad.reshape(key_rows.shape[0], -1).astype(jnp.bfloat16)
    return (key_grad, value_grad)


def spread(block, axis):
    size = lax.axis_size(axis)
    return lax.all_to_all(jnp.broadcast_to(block[None], (size,) + block.shape), axis, 0, 0)


def share_sum(blocks, axis):
    return jnp.sum(lax.all_to_all(blocks, axis, 0, 0).astype(jnp.float32), axis=0)


def swap(block):
    return lax.ppermute(block, "segment", [(0, 1), (1, 0)])


def to_chunks(block, parts):
    high, wide = (block.shape[0] // 8, block.shape[1] // 128)
    tiles = block.reshape(high, 8, wide, 128).transpose(0, 2, 1, 3).reshape(-1, 8, 128)
    each = -(-tiles.shape[0] // parts)
    tiles = jnp.pad(tiles, ((0, each * parts - tiles.shape[0]), (0, 0), (0, 0)))
    return tiles.reshape(parts, each, 8, 128)


def from_chunks(chunks, rows, cols):
    high, wide = (rows // 8, cols // 128)
    tiles = chunks.reshape(-1, 8, 128)[: high * wide]
    return tiles.reshape(high, wide, 8, 128).transpose(0, 2, 1, 3).reshape(rows, cols)


def shards(
    frames, dec_states, out_grad, frame_lengths, token_lengths, weights, norm_gains, norm_biases
):
    core = lax.axis_index("segment")
    first = core == 0
    own = weights[0]
    shard_rows, features = frames.shape[1:]
    mp = lax.axis_size("mp")
    dp = lax.axis_size("dp")
    head_cols = own.shape[1]
    rows = shard_rows * mp
    half = features // 2

    def mine(array):
        return lax.dynamic_index_in_dim(array, core, 0, keepdims=False)

    inputs = mine(frames)
    tokens = mine(dec_states)
    upstream = mine(out_grad)
    frame_ids = utterance_ids(mine(frame_lengths)[0], rows)
    token_ids = utterance_ids(mine(token_lengths)[0], tokens.shape[0])
    out_sent = lax.ppermute(own[3, :, half:], "segment", [(0, 1)])
    out_part = jnp.where(first, own[3, :, :half], out_sent)
    out_part = lax.all_gather(out_part, "mp", axis=0, tiled=True)
    out_rest = swap(out_part)
    enc_full = spread(inputs, "mp").reshape(rows, features)
    other = swap(own)
    enc = jnp.where(first, own, other)
    dec = jnp.where(first, other, own)
    normed = layer_norm(enc_full.astype(jnp.float32), norm_gains[0], norm_biases[0]).astype(
        jnp.bfloat16
    )
    queries = project(normed, enc[0])
    key_rows = project(normed, enc[1])
    value_rows = project(normed, enc[2])
    context, probs = attend(queries, key_rows, value_rows, frame_ids[:, None] == frame_ids[None, :])
    context_full = spread(context, "mp").transpose(1, 0, 2).reshape(rows, mp * head_cols)
    out_mine = jnp.dot(context_full, out_part, preferred_element_type=jnp.float32)
    out_other = jnp.dot(context_full, out_rest, preferred_element_type=jnp.float32)
    summed = jnp.concatenate(
        [jnp.where(first, out_mine, out_other), jnp.where(first, out_other, out_mine)], axis=1
    )
    states_full = (enc_full.astype(jnp.float32) + summed).astype(jnp.bfloat16)
    states = lax.dynamic_slice_in_dim(states_full, lax.axis_index("mp") * shard_rows, shard_rows, 0)
    state_normed = layer_norm(
        states_full.astype(jnp.float32), norm_gains[2], norm_biases[2]
    ).astype(jnp.bfloat16)
    token_normed = layer_norm(tokens.astype(jnp.float32), norm_gains[1], norm_biases[1]).astype(
        jnp.bfloat16
    )
    dec_queries = project(token_normed, dec[0])
    dec_keys = project(state_normed, dec[1])
    dec_values = project(state_normed, dec[2])
    dec_context, dec_probs = attend(
        dec_queries, dec_keys, dec_values, token_ids[:, None] == frame_ids[None, :]
    )
    grad_context = project(upstream, dec[3])
    dec_key_grad, dec_value_grad = attend_backward(
        dec_queries, dec_keys, dec_values, dec_probs, grad_context
    )
    partial = (
        jnp.dot(dec_key_grad, dec[1], preferred_element_type=jnp.float32)
        + jnp.dot(dec_value_grad, dec[2], preferred_element_type=jnp.float32)
    ).astype(jnp.bfloat16)

    def combine(term):
        left, right = (term[:, :half], term[:, half:])
        sent = swap(jnp.where(first, right, left).astype(jnp.bfloat16))
        return (jnp.where(first, left, right) + sent.astype(jnp.float32)).astype(jnp.bfloat16)

    def reduce_groups(term):
        total = share_sum(to_chunks(term, dp), "dp").astype(jnp.bfloat16)
        return from_chunks(spread(total, "dp"), 3 * head_cols, half)

    dec_term = jnp.concatenate(
        [
            outer_rows(dec_key_grad, state_normed),
            outer_rows(dec_value_grad, state_normed),
            outer_rows(dec_context, upstream),
        ]
    )
    pieces = lax.all_to_all(partial.reshape(mp, shard_rows, features), "mp", 0, 0)
    pieces, dec_part = lax.optimization_barrier((pieces, combine(dec_term)))
    dec_total = lax.psum(dec_part, "dp")
    summed = jnp.sum(pieces.astype(jnp.float32), axis=0)
    grads = norm_backward(summed, states.astype(jnp.float32), norm_gains[2]).astype(jnp.bfloat16)
    grads_full = spread(grads, "mp").reshape(rows, features)
    att_grad = project(grads_full, enc[3])
    enc_key_grad, enc_value_grad = attend_backward(queries, key_rows, value_rows, probs, att_grad)
    enc_term = jnp.concatenate(
        [
            outer_rows(enc_key_grad, normed),
            outer_rows(enc_value_grad, normed),
            outer_rows(context, grads_full),
        ]
    )
    enc_total = reduce_groups(combine(enc_term))
    kept = jnp.where(first, enc_total, dec_total)
    got = swap(jnp.where(first, dec_total, enc_total))
    gradient = jnp.concatenate(
        [jnp.where(first, kept, got), jnp.where(first, got, kept)], axis=1
    ).astype(jnp.float32)
    return gradient.reshape(1, 3, head_cols, features)


def solution(mesh):
    placed = (
        P(None, ("dp", "mp"), None),
        P(None, "dp", None),
        P(None, "dp", None),
        P(None, "dp", None),
        P(None, "dp", None),
        P("segment", None, "mp", None),
        P(),
        P(),
    )
    return jax.shard_map(
        shards,
        mesh=mesh,
        in_specs=placed,
        out_specs=P("segment", None, "mp", None),
        check_vma=False,
    )
```

profile of v0, /device:TPU:1, one launch (start us, length us, event | category | flops | bytes accessed | tf_op | source)
XLA Modules:
  0.0 379.2 jit_solution(9192799755561751875)
XLA Ops:
  6.6 1.0 dynamic-slice_bitcast_fusion
  7.6 0.9 broadcast_in_dim.31
  8.5 10.9 %all-to-all-start = ((bf16[8,32,1280]{2,1,0:T(8,128)(2,1)}), bf16[8,32,1280]{2,1,0:T(8,128)(2,1)S(1)}, u32[]{:S(2)}, u32[]{:S(2)}) async-start(bf16[8,32,1280]{2,1,0:T(8,128)(2,1)} %broadcast_in_dim.31), calls=%async_computation | async-start | bytes 1310720 | tf_op jit(solution)/shard_map/all_to_all | solution.py:104
  19.4 2.9 collective-permute-start
  22.3 1.3 collective-permute-start.1
  27.3 12.8 %all-to-all-done = bf16[8,32,1280]{2,1,0:T(8,128)(2,1)S(1)} async-done(((bf16[8,32,1280]{2,1,0:T(8,128)(2,1)}), bf16[8,32,1280]{2,1,0:T(8,128)(2,1)S(1)}, u32[]{:S(2)}, u32[]{:S(2)}) %all-to-all-start) | async-done | bytes 655392 | tf_op jit(solution)/shard_map/all_to_all | solution.py:104
  41.4 1.5 broadcast_select_fusion.1
  44.4 23.2 %all-gather.2.cloned.1.call-done = bf16[1024,640]{1,0:T(8,128)(2,1)} async-done(((bf16[128,640]{1,0:T(8,128)(2,1)}), bf16[1024,640]{1,0:T(8,128)(2,1)}) %all-gather.2.cloned.1.call-update) | async-done | bytes 1310736 | tf_op jit(solution)/shard_map/all_gather | solution.py:152
  67.6 7.2 %collective-permute-start.2 = (bf16[1024,640]{1,0:T(8,128)(2,1)}, bf16[1024,640]{1,0:T(8,128)(2,1)}, u32[]{:S(2)}, u32[]{:S(2)}) collective-permute-start(bf16[1024,640]{1,0:T(8,128)(2,1)} %all-gather.2.cloned.1.call-done), channel_id=1, source_target_pairs={{0,8},{8,0},{1,9},{9,1},{2,10},{10,2},{3,11},{11,3},{4,12},{12,4},... | collective-permute-start | bytes 3932168 | tf_op jit(solution)/shard_map/ppermute | solution.py:112
  74.8 1.2 fusion.70
  76.5 0.8 broadcast_in_dim.34
  77.4 3.9 %all-to-all-start.1 = ((bf16[8,256,128]{1,2,0:T(8,128)(2,1)}), bf16[8,256,128]{1,2,0:T(8,128)(2,1)S(1)}, u32[]{:S(2)}, u32[]{:S(2)}) async-start(bf16[8,256,128]{1,2,0:T(8,128)(2,1)} %broadcast_in_dim.34), calls=%async_computation.1 | async-start | bytes 1048576 | tf_op jit(solution)/shard_map/all_to_all | solution.py:104
  81.3 1.2 bitcast_convert_fusion
  82.5 0.9 convolution_convert_fusion.11
  83.4 1.4 copy.34
  84.8 0.8 convolution_convert_fusion.10
  85.7 1.4 copy.35
  87.1 12.2 %all-to-all-done.1 = bf16[8,256,128]{1,2,0:T(8,128)(2,1)S(1)} async-done(((bf16[8,256,128]{1,2,0:T(8,128)(2,1)}), bf16[8,256,128]{1,2,0:T(8,128)(2,1)S(1)}, u32[]{:S(2)}, u32[]{:S(2)}) %all-to-all-start.1) | async-done | bytes 524320 | tf_op jit(solution)/shard_map/all_to_all | solution.py:104
  99.3 1.9 fusion.72
  101.2 1.9 broadcast_select_fusion.7
  106.2 1.1 fusion.74
  107.3 2.4 fusion.25
  110.2 0.9 multiply_reduce_fusion.3
  111.0 1.3 fusion.17
  112.4 1.1 fusion.73
  113.5 1.1 fusion.42
  114.6 2.2 fusion.2
  116.8 3.5 all-to-all-start.2
  120.3 1.6 pad_maximum_fusion
  122.0 2.4 collective-permute-start.3
  124.4 1.0 convert_reduce_fusion.4
  125.9 1.0 add_convert_fusion.2
  126.9 14.1 %all-to-all-done.2 = bf16[8,32,1280]{2,1,0:T(8,128)(2,1)S(1)} async-done(((bf16[8,32,1280]{2,1,0:T(8,128)(2,1)}), bf16[8,32,1280]{2,1,0:T(8,128)(2,1)S(1)}, u32[]{:S(2)}, u32[]{:S(2)}) %all-to-all-start.2) | async-done | bytes 655392 | tf_op jit(solution)/shard_map/all_to_all | solution.py:210
  141.5 22.3 %all_to_all.30 = bf16[8,32,1280]{2,1,0:T(8,128)(2,1)S(1)} all-to-all(bf16[8,32,1280]{2,1,0:T(8,128)(2,1)S(1)} %broadcast_in_dim.37), channel_id=1, replica_groups=mesh['dp'=32,'segment'=2,'mp'=8] {'mp'}, dimensions={0} | all-to-all | bytes 1310720 | tf_op jit(solution)/shard_map/all_to_all | solution.py:104
  163.8 1.4 convolution_convert_fusion
  165.5 1.5 convolution_convert_fusion.7
  167.3 1.4 fusion.16
  169.5 3.2 collective-permute-start.4
  172.7 1.5 collective-permute-done.4
  174.4 23.2 %all_to_all.31 = bf16[32,8,8,128]{3,2,1,0:T(8,128)(2,1)S(1)} all-to-all(bf16[32,8,8,128]{3,2,1,0:T(8,128)(2,1)S(1)} %bitcast.176), channel_id=1, replica_groups=mesh['dp'=32,'segment'=2,'mp'=8] {'dp'}, dimensions={0} | all-to-all | bytes 1048576 | tf_op jit(solution)/shard_map/all_to_all | solution.py:108
  197.7 0.9 broadcast_in_dim.42
  198.6 8.1 %all-to-all-start.5 = ((bf16[32,8,8,128]{3,2,1,0:T(8,128)(2,1)}), bf16[32,8,8,128]{3,2,1,0:T(8,128)(2,1)S(1)}, u32[]{:S(2)}, u32[]{:S(2)}) async-start(bf16[32,8,8,128]{3,2,1,0:T(8,128)(2,1)} %broadcast_in_dim.42), calls=%async_computation.5 | async-start | bytes 1048576 | tf_op jit(solution)/shard_map/all_to_all | solution.py:104
  206.8 0.7 all-reduce.3.cloned.1.call-update
  207.5 13.3 %all-to-all-done.5 = bf16[32,8,8,128]{3,2,1,0:T(8,128)(2,1)S(1)} async-done(((bf16[32,8,8,128]{3,2,1,0:T(8,128)(2,1)}), bf16[32,8,8,128]{3,2,1,0:T(8,128)(2,1)S(1)}, u32[]{:S(2)}, u32[]{:S(2)}) %all-to-all-start.5) | async-done | bytes 524320 | tf_op jit(solution)/shard_map/all_to_all | solution.py:104
  220.8 140.2 %all-reduce.3.cloned.1.call-done = bf16[384,640]{1,0:T(8,128)(2,1)} async-done(((bf16[384,640]{1,0:T(8,128)(2,1)}), bf16[384,640]{1,0:T(8,128)(2,1)}) %all-reduce.3.cloned.1.call-update) | async-done | bytes 491536 | tf_op jit(solution)/shard_map/psum | solution.py:212
  361.1 8.2 %collective-permute-start.5 = (bf16[384,640]{1,0:T(8,128)(2,1)S(1)}, bf16[384,640]{1,0:T(8,128)(2,1)S(1)}, u32[]{:S(2)}, u32[]{:S(2)}) collective-permute-start(bf16[384,640]{1,0:T(8,128)(2,1)S(1)} %broadcast_select_fusion.4), channel_id=1, source_target_pairs={{0,8},{8,0},{1,9},{9,1},{2,10},{10,2},{3,11},{11,3},{4,12},{12,4},... | collective-permute-start | bytes 1474568 | tf_op jit(solution)/shard_map/ppermute | solution.py:112
  369.3 1.5 collective-permute-done.5
  370.9 1.4 maximum_convert_fusion
  (126 shorter events, 13.2 us)
Async XLA Ops:
  6.5 78.3 %copy-start = (bf16[2,64,1280]{2,1,0:T(8,128)(2,1)S(1)}, bf16[2,64,1280]{2,1,0:T(8,128)(2,1)}, u32[]{:S(2)}) copy-start(bf16[2,64,1280]{2,1,0:T(8,128)(2,1)} %param.10) | copy-start | bytes 983044
  6.5 12.9 %copy-start.4 = (bf16[1,4,128,1280]{3,2,1,0:T(8,128)(2,1)S(1)}, bf16[1,4,128,1280]{3,2,1,0:T(8,128)(2,1)}, u32[]{:S(2)}) copy-start(bf16[1,4,128,1280]{3,2,1,0:T(8,128)(2,1)} %param.13) | copy-start | bytes 3932164
  6.5 17.1 %copy-start.20 = (s32[2,1,4]{2,1,0:T(1,128)S(1)}, s32[2,1,4]{2,1,0:T(1,128)}, u32[]{:S(2)}) copy-start(s32[2,1,4]{2,1,0:T(1,128)} %param.11) | copy-start | bytes 100
  6.5 17.1 %copy-start.21 = (s32[2,1,4]{2,1,0:T(1,128)S(1)}, s32[2,1,4]{2,1,0:T(1,128)}, u32[]{:S(2)}) copy-start(s32[2,1,4]{2,1,0:T(1,128)} %param.12) | copy-start | bytes 100
  6.5 17.4 %copy-start.8 = (bf16[2,64,1280]{2,1,0:T(8,128)(2,1)S(1)}, bf16[2,64,1280]{2,1,0:T(8,128)(2,1)}, u32[]{:S(2)}) copy-start(bf16[2,64,1280]{2,1,0:T(8,128)(2,1)} %param.9) | copy-start | bytes 983044
  7.6 18.3 %copy-start.14 = (f32[3,1280]{1,0:T(4,128)S(1)}, f32[3,1280]{1,0:T(4,128)}, u32[]{:S(2)}) copy-start(f32[3,1280]{1,0:T(4,128)} %param.15) | copy-start | bytes 46084
  7.6 18.3 %copy-start.15 = (f32[3,1280]{1,0:T(4,128)S(1)}, f32[3,1280]{1,0:T(4,128)}, u32[]{:S(2)}) copy-start(f32[3,1280]{1,0:T(4,128)} %param.14) | copy-start | bytes 46084
  8.5 31.6 %all-to-all-start = ((bf16[8,32,1280]{2,1,0:T(8,128)(2,1)}), bf16[8,32,1280]{2,1,0:T(8,128)(2,1)S(1)}, u32[]{:S(2)}, u32[]{:S(2)}) async-start(bf16[8,32,1280]{2,1,0:T(8,128)(2,1)} %broadcast_in_dim.31), calls=%async_computation | async-start | bytes 1310720 | tf_op jit(solution)/shard_map/all_to_all | solution.py:104
  19.3 48.2 %all-gather.2.cloned.1.call-start = ((), (), s32[]{:S(2)}) async-start(), calls=%async_computation.6 | async-start | bytes 1474560 | tf_op jit(solution)/shard_map/all_gather | solution.py:152
  19.4 21.6 %collective-permute-start = (bf16[4,128,1280]{2,1,0:T(8,128)(2,1)S(1)}, bf16[4,128,1280]{2,1,0:T(8,128)(2,1)}, u32[]{:S(2)}, u32[]{:S(2)}) collective-permute-start(bf16[4,128,1280]{2,1,0:T(8,128)(2,1)S(1)} %bitcast.177), channel_id=1, source_target_pairs={{0,8},{8,0},{1,9},{9,1},{2,10},{10,2},{3,11},{11,3},{4,12},{12,4},... | collective-permute-start | bytes 3932168 | tf_op jit(solution)/shard_map/ppermute | solution.py:112
  22.3 4.3 %collective-permute-start.1 = (bf16[128,640]{1,0:T(8,128)(2,1)S(1)}, bf16[128,640]{1,0:T(8,128)(2,1)S(1)}, u32[]{:S(2)}, u32[]{:S(2)}) collective-permute-start(bf16[128,640]{1,0:T(8,128)(2,1)S(1)} %slice_bitcast_fusion.18), channel_id=1, source_target_pairs={{0,8},{1,9},{2,10},{3,11},{4,12},{5,13},{6,14},{7,15},{16,24},{17,... | collective-permute-start | bytes 491528 | tf_op jit(solution)/shard_map/ppermute | solution.py:150
  24.0 1.9 copy-start.18
  25.3 50.7 %copy-start.10 = (pred[256,256]{0,1:T(8,128)(4,1)}, pred[256,256]{0,1:T(8,128)(4,1)S(1)}, u32[]{:S(2)}) copy-start(pred[256,256]{0,1:T(8,128)(4,1)S(1)} %broadcast_compare_fusion) | copy-start | bytes 196612
  40.1 1.3 copy-start.5
  42.9 1.1 copy-start.7
  42.9 41.9 %copy-start.2 = (bf16[4,128,1280]{2,1,0:T(8,128)(2,1)}, bf16[4,128,1280]{2,1,0:T(8,128)(2,1)S(1)}, u32[]{:S(2)}) copy-start(bf16[4,128,1280]{2,1,0:T(8,128)(2,1)S(1)} %get-tuple-element.22) | copy-start | bytes 3932164
  43.3 32.7 %copy-start.22 = (bf16[256,128]{0,1:T(8,128)(2,1)}, bf16[256,128]{0,1:T(8,128)(2,1)S(1)}, u32[]{:S(2)}) copy-start(bf16[256,128]{0,1:T(8,128)(2,1)S(1)} %convolution_convert_fusion.5) | copy-start | bytes 196612
  44.0 32.5 %copy-start.24 = (bf16[256,128]{0,1:T(8,128)(2,1)}, bf16[256,128]{0,1:T(8,128)(2,1)S(1)}, u32[]{:S(2)}) copy-start(bf16[256,128]{0,1:T(8,128)(2,1)S(1)} %convolution_convert_fusion.6) | copy-start | bytes 196612
  44.3 32.2 %copy-start.26 = (bf16[256,128]{0,1:T(8,128)(2,1)}, bf16[256,128]{0,1:T(8,128)(2,1)S(1)}, u32[]{:S(2)}) copy-start(bf16[256,128]{0,1:T(8,128)(2,1)S(1)} %convolution_convert_fusion.4) | copy-start | bytes 196612
  67.6 31.7 %collective-permute-start.2 = (bf16[1024,640]{1,0:T(8,128)(2,1)}, bf16[1024,640]{1,0:T(8,128)(2,1)}, u32[]{:S(2)}, u32[]{:S(2)}) collective-permute-start(bf16[1024,640]{1,0:T(8,128)(2,1)} %all-gather.2.cloned.1.call-done), channel_id=1, source_target_pairs={{0,8},{8,0},{1,9},{9,1},{2,10},{10,2},{3,11},{11,3},{4,12},{12,4},... | collective-permute-start | bytes 3932168 | tf_op jit(solution)/shard_map/ppermute | solution.py:112
  76.0 1.4 copy-start.30
  77.4 21.9 %all-to-all-start.1 = ((bf16[8,256,128]{1,2,0:T(8,128)(2,1)}), bf16[8,256,128]{1,2,0:T(8,128)(2,1)S(1)}, u32[]{:S(2)}, u32[]{:S(2)}) async-start(bf16[8,256,128]{1,2,0:T(8,128)(2,1)} %broadcast_in_dim.34), calls=%async_computation.1 | async-start | bytes 1048576 | tf_op jit(solution)/shard_map/all_to_all | solution.py:104
  81.2 1.3 copy-start.9
  81.2 1.3 copy-start.16
  81.2 1.2 copy-start.17
  81.3 1.2 copy-start.19
  81.3 1.2 copy-start.28
  103.3 1.3 copy-start.3
  104.0 1.4 copy-start.11
  104.0 1.4 copy-start.13
  104.0 1.7 copy-start.12
  112.4 2.2 copy-start.1
  116.8 24.2 %all-to-all-start.2 = ((bf16[8,32,1280]{2,1,0:T(8,128)(2,1)}), bf16[8,32,1280]{2,1,0:T(8,128)(2,1)S(1)}, u32[]{:S(2)}, u32[]{:S(2)}) async-start(bf16[8,32,1280]{2,1,0:T(8,128)(2,1)} %bitcast.37), calls=%async_computation.2 | async-start | bytes 1310720 | tf_op jit(solution)/shard_map/all_to_all | solution.py:210
  122.0 3.9 %collective-permute-start.3 = (bf16[384,640]{1,0:T(8,128)(2,1)S(1)}, bf16[384,640]{1,0:T(8,128)(2,1)S(1)}, u32[]{:S(2)}, u32[]{:S(2)}) collective-permute-start(bf16[384,640]{1,0:T(8,128)(2,1)S(1)} %select_convert_fusion.1), channel_id=1, source_target_pairs={{0,8},{8,0},{1,9},{9,1},{2,10},{10,2},{3,11},{11,3},{4,12},{12,4},... | collective-permute-start | bytes 1474568 | tf_op jit(solution)/shard_map/ppermute | solution.py:112
  163.8 1.7 copy-start.23
  163.8 1.7 copy-start.25
  163.8 1.7 copy-start.31
  165.4 1.5 copy-start.27
  165.5 1.5 copy-start.29
  169.5 4.7 %collective-permute-start.4 = (bf16[384,640]{1,0:T(8,128)(2,1)S(1)}, bf16[384,640]{1,0:T(8,128)(2,1)S(1)}, u32[]{:S(2)}, u32[]{:S(2)}) collective-permute-start(bf16[384,640]{1,0:T(8,128)(2,1)S(1)} %select_convert_fusion), channel_id=1, source_target_pairs={{0,8},{8,0},{1,9},{9,1},{2,10},{10,2},{3,11},{11,3},{4,12},{12,4},... | collective-permute-start | bytes 1474568 | tf_op jit(solution)/shard_map/ppermute | solution.py:112
  198.6 22.2 %all-to-all-start.5 = ((bf16[32,8,8,128]{3,2,1,0:T(8,128)(2,1)}), bf16[32,8,8,128]{3,2,1,0:T(8,128)(2,1)S(1)}, u32[]{:S(2)}, u32[]{:S(2)}) async-start(bf16[32,8,8,128]{3,2,1,0:T(8,128)(2,1)} %broadcast_in_dim.42), calls=%async_computation.5 | async-start | bytes 1048576 | tf_op jit(solution)/shard_map/all_to_all | solution.py:104
  206.7 154.3 %all-reduce.3.cloned.1.call-start = ((), (), s32[]{:S(2)}) async-start(), calls=%async_computation.7 | async-start | bytes 983040 | tf_op jit(solution)/shard_map/psum | solution.py:212
  361.0 9.8 %copy-start.6 = (bf16[384,640]{1,0:T(8,128)(2,1)S(1)}, bf16[384,640]{1,0:T(8,128)(2,1)}, u32[]{:S(2)}) copy-start(bf16[384,640]{1,0:T(8,128)(2,1)} %all-reduce.3.cloned.1.call-done) | copy-start | bytes 1474564
  361.1 9.7 %collective-permute-start.5 = (bf16[384,640]{1,0:T(8,128)(2,1)S(1)}, bf16[384,640]{1,0:T(8,128)(2,1)S(1)}, u32[]{:S(2)}, u32[]{:S(2)}) collective-permute-start(bf16[384,640]{1,0:T(8,128)(2,1)S(1)} %broadcast_select_fusion.4), channel_id=1, source_target_pairs={{0,8},{8,0},{1,9},{9,1},{2,10},{10,2},{3,11},{11,3},{4,12},{12,4},... | collective-permute-start | bytes 1474568 | tf_op jit(solution)/shard_map/ppermute | solution.py:112
Sparse Core Ops, SparseCore 0:
  27.4 40.0 all-gather.1
  210.9 150.0 all-reduce.2
where the time goes:
time: 380 us; the launch traced here: 379 us
  waiting for transfers between devices  220 us (58%)
  starting transfers between devices  51.7 us (14%)
  blocking collectives  45.5 us (12%)
  matrix products  25.7 us (7%)
  between operations  14 us (4%)
  other arithmetic  13.8 us (4%)
  local copies, waits for them, and re-layouts  8.81 us (2%)
    psum x1, waiting for transfers between devices, shards(): dec_total = lax.psum(dec_part, 'dp')  140 us
    all_to_all x3, waiting for transfers between devices, spread(): lax.all_to_all(jnp.broadcast_to(block[None], (size,) + block.shape), axis...  38.3 us
    ppermute x5, starting transfers between devices, swap(): return lax.ppermute(block, 'segment', [(0, 1), (1, 0)])  23.9 us
    all_to_all x1, blocking collectives, share_sum(): lax.all_to_all(blocks, axis, 0, 0).astype(jnp.float32)  23.2 us
    all_gather x1, waiting for transfers between devices, shards(): out_part = lax.all_gather(out_part, 'mp', axis=0, tiled=True)  23.2 us
    all_to_all x3, starting transfers between devices, spread(): lax.all_to_all(jnp.broadcast_to(block[None], (size,) + block.shape), axis...  22.8 us
    all_to_all x1, blocking collectives, spread(): lax.all_to_all(jnp.broadcast_to(block[None], (size,) + block.shape), axis...  22.3 us
    all_to_all x1, waiting for transfers between devices, shards(): lax.all_to_all(partial.reshape(mp, shard_rows, features), 'mp', 0, 0)  14.1 us
  transfers between devices with their start and end apart: 12, of which 9 were waited for; matrix products, arithmetic and copies ran while one was open for 5% of the time, Pallas kernels for 0%

commit v1 on v0

--- a/solution.py
+++ b/solution.py
@@ -209,7 +209,7 @@
     )
     pieces = lax.all_to_all(partial.reshape(mp, shard_rows, features), "mp", 0, 0)
     pieces, dec_part = lax.optimization_barrier((pieces, combine(dec_term)))
-    dec_total = lax.psum(dec_part, "dp")
+    dec_total = jnp.sum(lax.all_gather(dec_part, "dp"), axis=0)
     summed = jnp.sum(pieces.astype(jnp.float32), axis=0)
     grads = norm_backward(summed, states.astype(jnp.float32), norm_gains[2]).astype(jnp.bfloat16)
     grads_full = spread(grads, "mp").reshape(rows, features)

time: 380 us -> 312 us (0.82)
  waiting for transfers between devices: 220 us -> 124 us
  blocking collectives: 45.5 us -> 72.1 us
  starting transfers between devices: 51.7 us -> 40.5 us
  other arithmetic: 13.8 us -> 23.8 us
    psum x1 -> x0, waiting for transfers between devices: 140 us -> none  [shards(): dec_total = lax.psum(dec_part, 'dp')]
    all_gather x0 -> x1, waiting for transfers between devices: none -> 60.9 us  [shards(): dec_total = jnp.sum(lax.all_gather(dec_part, 'dp'), axis=0)]
    all_to_all x1 -> x2, blocking collectives: 22.3 us -> 48.9 us  [spread(): lax.all_to_all(jnp.broadcast_to(block[None], (size,) + block.shape), axis...]
    all_to_all x3 -> x2, waiting for transfers between devices: 38.3 us -> 22.8 us  [spread(): lax.all_to_all(jnp.broadcast_to(block[None], (size,) + block.shape), axis...]
    reduce_sum x0 -> x1, other arithmetic: none -> 8.43 us  [shards(): dec_total = jnp.sum(lax.all_gather(dec_part, 'dp'), axis=0)]
    all_to_all x3 -> x2, starting transfers between devices: 22.8 us -> 14.7 us  [spread(): lax.all_to_all(jnp.broadcast_to(block[None], (size,) + block.shape), axis...]
  transfers between devices with their start and end apart: 12 -> 11, of which waited for: 9 -> 8; matrix products, arithmetic and copies ran while one was open for 5% -> 9% of each run, Pallas kernels for 0% -> 0%
where the time goes in v1:
time: 312 us; the launch traced here: 311 us
  waiting for transfers between devices  124 us (40%)
  blocking collectives  72.1 us (23%)
  starting transfers between devices  40.5 us (13%)
  matrix products  28.9 us (9%)
  other arithmetic  23.8 us (8%)
  between operations  14 us (4%)
  local copies, waits for them, and re-layouts  7.94 us (3%)
    all_gather x1, waiting for transfers between devices, shards(): dec_total = jnp.sum(lax.all_gather(dec_part, 'dp'), axis=0)  60.9 us
    all_to_all x2, blocking collectives, spread(): lax.all_to_all(jnp.broadcast_to(block[None], (size,) + block.shape), axis...  48.9 us
    all_to_all x1, blocking collectives, share_sum(): lax.all_to_all(blocks, axis, 0, 0).astype(jnp.float32)  23.2 us
    all_gather x1, waiting for transfers between devices, shards(): out_part = lax.all_gather(out_part, 'mp', axis=0, tiled=True)  23 us
    all_to_all x2, waiting for transfers between devices, spread(): lax.all_to_all(jnp.broadcast_to(block[None], (size,) + block.shape), axis...  22.8 us
    ppermute x5, starting transfers between devices, swap(): return lax.ppermute(block, 'segment', [(0, 1), (1, 0)])  20.2 us
    all_to_all x2, starting transfers between devices, spread(): lax.all_to_all(jnp.broadcast_to(block[None], (size,) + block.shape), axis...  14.7 us
    all_to_all x1, waiting for transfers between devices, shards(): lax.all_to_all(partial.reshape(mp, shard_rows, features), 'mp', 0, 0)  12.5 us
  transfers between devices with their start and end apart: 11, of which 8 were waited for; matrix products, arithmetic and copies ran while one was open for 9% of the time, Pallas kernels for 0%

profile of v1, /device:TPU:1, one launch (start us, length us, event | category | flops | bytes accessed | tf_op | source)
XLA Modules:
  0.0 310.9 jit_solution(10801803753165273172)
XLA Ops:
  6.6 1.0 dynamic-slice_bitcast_fusion
  7.6 0.9 broadcast_in_dim.31
  8.5 10.9 %all-to-all-start = ((bf16[8,32,1280]{2,1,0:T(8,128)(2,1)}), bf16[8,32,1280]{2,1,0:T(8,128)(2,1)S(1)}, u32[]{:S(2)}, u32[]{:S(2)}) async-start(bf16[8,32,1280]{2,1,0:T(8,128)(2,1)} %broadcast_in_dim.31), calls=%async_computation | async-start | bytes 1310720 | tf_op jit(solution)/shard_map/all_to_all | solution.py:104
  19.4 2.9 collective-permute-start
  22.3 1.3 collective-permute-start.1
  25.6 0.8 fusion.24
  27.1 13.1 %all-to-all-done = bf16[8,32,1280]{2,1,0:T(8,128)(2,1)S(1)} async-done(((bf16[8,32,1280]{2,1,0:T(8,128)(2,1)}), bf16[8,32,1280]{2,1,0:T(8,128)(2,1)S(1)}, u32[]{:S(2)}, u32[]{:S(2)}) %all-to-all-start) | async-done | bytes 655392 | tf_op jit(solution)/shard_map/all_to_all | solution.py:104
  41.4 1.5 broadcast_select_fusion.1
  44.4 23.0 %all-gather.4.cloned.1.call-done = bf16[1024,640]{1,0:T(8,128)(2,1)} async-done(((bf16[128,640]{1,0:T(8,128)(2,1)}), bf16[1024,640]{1,0:T(8,128)(2,1)}) %all-gather.4.cloned.1.call-update) | async-done | bytes 1310736 | tf_op jit(solution)/shard_map/all_gather | solution.py:152
  67.3 7.2 %collective-permute-start.2 = (bf16[1024,640]{1,0:T(8,128)(2,1)}, bf16[1024,640]{1,0:T(8,128)(2,1)}, u32[]{:S(2)}, u32[]{:S(2)}) collective-permute-start(bf16[1024,640]{1,0:T(8,128)(2,1)} %all-gather.4.cloned.1.call-done), channel_id=1, source_target_pairs={{0,8},{8,0},{1,9},{9,1},{2,10},{10,2},{3,11},{11,3},{4,12},{12,4},... | collective-permute-start | bytes 3932168 | tf_op jit(solution)/shard_map/ppermute | solution.py:112
  74.6 1.2 fusion.70
  76.3 0.8 broadcast_in_dim.34
  77.1 3.9 %all-to-all-start.1 = ((bf16[8,256,128]{1,2,0:T(8,128)(2,1)}), bf16[8,256,128]{1,2,0:T(8,128)(2,1)S(1)}, u32[]{:S(2)}, u32[]{:S(2)}) async-start(bf16[8,256,128]{1,2,0:T(8,128)(2,1)} %broadcast_in_dim.34), calls=%async_computation.1 | async-start | bytes 1048576 | tf_op jit(solution)/shard_map/all_to_all | solution.py:104
  82.4 1.3 broadcast_compare_fusion.1
  83.7 1.8 convolution_convert_fusion.11
  85.6 1.4 copy.34
  87.0 0.8 convolution_convert_fusion.10
  87.8 1.4 copy.35
  89.2 9.7 %all-to-all-done.1 = bf16[8,256,128]{1,2,0:T(8,128)(2,1)S(1)} async-done(((bf16[8,256,128]{1,2,0:T(8,128)(2,1)}), bf16[8,256,128]{1,2,0:T(8,128)(2,1)S(1)}, u32[]{:S(2)}, u32[]{:S(2)}) %all-to-all-start.1) | async-done | bytes 524320 | tf_op jit(solution)/shard_map/all_to_all | solution.py:104
  99.0 1.9 fusion.72
  100.9 1.9 broadcast_select_fusion.7
  106.0 2.2 fusion.74
  108.2 2.4 fusion.25
  111.0 0.9 multiply_reduce_fusion.3
  111.9 1.3 fusion.17
  113.3 2.3 fusion.73
  115.6 1.1 fusion.42
  116.6 2.2 fusion.2
  118.8 4.2 %all-to-all-start.2 = ((bf16[8,32,1280]{2,1,0:T(8,128)(2,1)}), bf16[8,32,1280]{2,1,0:T(8,128)(2,1)}, u32[]{:S(2)}, u32[]{:S(2)}) async-start(bf16[8,32,1280]{2,1,0:T(8,128)(2,1)} %bitcast.176), calls=%async_computation.2 | async-start | bytes 1310720 | tf_op jit(solution)/shard_map/all_to_all | solution.py:210
  123.0 1.6 pad_maximum_fusion
  124.8 2.4 collective-permute-start.3
  127.1 1.5 collective-permute-done.3
  128.6 0.9 add_convert_fusion.2
  129.6 12.5 %all-to-all-done.2 = bf16[8,32,1280]{2,1,0:T(8,128)(2,1)} async-done(((bf16[8,32,1280]{2,1,0:T(8,128)(2,1)}), bf16[8,32,1280]{2,1,0:T(8,128)(2,1)}, u32[]{:S(2)}, u32[]{:S(2)}) %all-to-all-start.2) | async-done | bytes 655392 | tf_op jit(solution)/shard_map/all_to_all | solution.py:210
  142.6 1.2 convert_reduce_fusion.1
  144.2 21.0 %all_to_all.30 = bf16[8,32,1280]{2,1,0:T(8,128)(2,1)S(1)} all-to-all(bf16[8,32,1280]{2,1,0:T(8,128)(2,1)S(1)} %broadcast_in_dim.37), channel_id=1, replica_groups=mesh['dp'=32,'segment'=2,'mp'=8] {'mp'}, dimensions={0} | all-to-all | bytes 1310720 | tf_op jit(solution)/shard_map/all_to_all | solution.py:104
  165.2 1.3 convolution_convert_fusion
  166.6 1.5 convolution_convert_fusion.7
  168.3 1.4 fusion.16
  170.8 5.1 %collective-permute-start.4 = (bf16[384,640]{1,0:T(8,128)(2,1)S(1)}, bf16[384,640]{1,0:T(8,128)(2,1)S(1)}, u32[]{:S(2)}, u32[]{:S(2)}) collective-permute-start(bf16[384,640]{1,0:T(8,128)(2,1)S(1)} %select_convert_fusion), channel_id=1, source_target_pairs={{0,8},{8,0},{1,9},{9,1},{2,10},{10,2},{3,11},{11,3},{4,12},{12,4},... | collective-permute-start | bytes 1474568 | tf_op jit(solution)/shard_map/ppermute | solution.py:112
  176.0 1.5 collective-permute-done.4
  177.6 23.2 %all_to_all.31 = bf16[32,8,8,128]{3,2,1,0:T(8,128)(2,1)S(1)} all-to-all(bf16[32,8,8,128]{3,2,1,0:T(8,128)(2,1)S(1)} %bitcast.179), channel_id=1, replica_groups=mesh['dp'=32,'segment'=2,'mp'=8] {'dp'}, dimensions={0} | all-to-all | bytes 1048576 | tf_op jit(solution)/shard_map/all_to_all | solution.py:108
  201.0 27.9 %all_to_all.32 = bf16[32,8,8,128]{3,2,1,0:T(8,128)(2,1)S(1)} all-to-all(bf16[32,8,8,128]{3,2,1,0:T(8,128)(2,1)S(1)} %broadcast_in_dim.42), channel_id=1, replica_groups=mesh['dp'=32,'segment'=2,'mp'=8] {'dp'}, dimensions={0} | all-to-all | bytes 1048576 | tf_op jit(solution)/shard_map/all_to_all | solution.py:104
  229.0 60.9 %all-gather.6.cloned.1.call-done = bf16[12288,640]{1,0:T(8,128)(2,1)} async-done(((bf16[384,640]{1,0:T(8,128)(2,1)}), bf16[12288,640]{1,0:T(8,128)(2,1)}) %all-gather.6.cloned.1.call-update) | async-done | bytes 15728656 | tf_op jit(solution)/shard_map/all_gather | solution.py:212
  289.9 8.4 %reduce_sum.195 = bf16[384,640]{1,0:T(8,128)(2,1)S(1)} reduce(bf16[32,384,640]{2,1,0:T(8,128)(2,1)} %bitcast.160, bf16[]{:T(256)} %constant.67.clone.1), dimensions={0}, to_apply=%region_22.23 | reduce | flops 7618560 | bytes 16220162 | tf_op jit(solution)/shard_map/reduce_sum | solution.py:212
  298.4 2.6 collective-permute-start.5
  301.0 1.5 collective-permute-done.5
  302.6 1.4 maximum_convert_fusion
  (118 shorter events, 13.7 us)
Async XLA Ops:
  6.5 80.5 %copy-start = (bf16[2,64,1280]{2,1,0:T(8,128)(2,1)S(1)}, bf16[2,64,1280]{2,1,0:T(8,128)(2,1)}, u32[]{:S(2)}) copy-start(bf16[2,64,1280]{2,1,0:T(8,128)(2,1)} %param.10) | copy-start | bytes 983044
  6.5 12.9 %copy-start.5 = (bf16[1,4,128,1280]{3,2,1,0:T(8,128)(2,1)S(1)}, bf16[1,4,128,1280]{3,2,1,0:T(8,128)(2,1)}, u32[]{:S(2)}) copy-start(bf16[1,4,128,1280]{3,2,1,0:T(8,128)(2,1)} %param.13) | copy-start | bytes 3932164
  6.5 17.1 %copy-start.17 = (s32[2,1,4]{2,1,0:T(1,128)S(1)}, s32[2,1,4]{2,1,0:T(1,128)}, u32[]{:S(2)}) copy-start(s32[2,1,4]{2,1,0:T(1,128)} %param.11) | copy-start | bytes 100
  6.5 17.1 %copy-start.18 = (s32[2,1,4]{2,1,0:T(1,128)S(1)}, s32[2,1,4]{2,1,0:T(1,128)}, u32[]{:S(2)}) copy-start(s32[2,1,4]{2,1,0:T(1,128)} %param.12) | copy-start | bytes 100
  6.5 17.3 %copy-start.8 = (bf16[2,64,1280]{2,1,0:T(8,128)(2,1)S(1)}, bf16[2,64,1280]{2,1,0:T(8,128)(2,1)}, u32[]{:S(2)}) copy-start(bf16[2,64,1280]{2,1,0:T(8,128)(2,1)} %param.9) | copy-start | bytes 983044
  7.6 16.6 %copy-start.13 = (f32[3,1280]{1,0:T(4,128)S(1)}, f32[3,1280]{1,0:T(4,128)}, u32[]{:S(2)}) copy-start(f32[3,1280]{1,0:T(4,128)} %param.15) | copy-start | bytes 46084
  7.6 16.6 %copy-start.14 = (f32[3,1280]{1,0:T(4,128)S(1)}, f32[3,1280]{1,0:T(4,128)}, u32[]{:S(2)}) copy-start(f32[3,1280]{1,0:T(4,128)} %param.14) | copy-start | bytes 46084
  8.5 31.6 %all-to-all-start = ((bf16[8,32,1280]{2,1,0:T(8,128)(2,1)}), bf16[8,32,1280]{2,1,0:T(8,128)(2,1)S(1)}, u32[]{:S(2)}, u32[]{:S(2)}) async-start(bf16[8,32,1280]{2,1,0:T(8,128)(2,1)} %broadcast_in_dim.31), calls=%async_computation | async-start | bytes 1310720 | tf_op jit(solution)/shard_map/all_to_all | solution.py:104
  19.3 48.0 %all-gather.4.cloned.1.call-start = ((), (), s32[]{:S(2)}) async-start(), calls=%async_computation.6 | async-start | bytes 1474560 | tf_op jit(solution)/shard_map/all_gather | solution.py:152
  19.4 21.6 %collective-permute-start = (bf16[4,128,1280]{2,1,0:T(8,128)(2,1)S(1)}, bf16[4,128,1280]{2,1,0:T(8,128)(2,1)}, u32[]{:S(2)}, u32[]{:S(2)}) collective-permute-start(bf16[4,128,1280]{2,1,0:T(8,128)(2,1)S(1)} %bitcast.180), channel_id=1, source_target_pairs={{0,8},{8,0},{1,9},{9,1},{2,10},{10,2},{3,11},{11,3},{4,12},{12,4},... | collective-permute-start | bytes 3932168 | tf_op jit(solution)/shard_map/ppermute | solution.py:112
  22.3 4.1 %collective-permute-start.1 = (bf16[128,640]{1,0:T(8,128)(2,1)S(1)}, bf16[128,640]{1,0:T(8,128)(2,1)S(1)}, u32[]{:S(2)}, u32[]{:S(2)}) collective-permute-start(bf16[128,640]{1,0:T(8,128)(2,1)S(1)} %slice_bitcast_fusion.18), channel_id=1, source_target_pairs={{0,8},{1,9},{2,10},{3,11},{4,12},{5,13},{6,14},{7,15},{16,24},{17,... | collective-permute-start | bytes 491528 | tf_op jit(solution)/shard_map/ppermute | solution.py:150
  24.0 16.1 %copy-start.15 = (s32[256]{0:T(256)}, s32[256]{0:T(256)S(1)}, u32[]{:S(2)}) copy-start(s32[256]{0:T(256)S(1)} %convert_reduce_fusion.5) | copy-start | bytes 3076
  24.0 16.9 %copy-start.16 = (f32[64]{0:T(128)}, f32[64]{0:T(128)S(1)}, u32[]{:S(2)}) copy-start(f32[64]{0:T(128)S(1)} %broadcast_multiply_fusion.2) | copy-start | bytes 772
  24.2 51.6 %copy-start.9 = (pred[256,256]{0,1:T(8,128)(4,1)}, pred[256,256]{0,1:T(8,128)(4,1)S(1)}, u32[]{:S(2)}) copy-start(pred[256,256]{0,1:T(8,128)(4,1)S(1)} %broadcast_compare_fusion) | copy-start | bytes 196612
  40.1 1.3 copy-start.6
  42.9 1.1 copy-start.7
  42.9 44.0 %copy-start.3 = (bf16[4,128,1280]{2,1,0:T(8,128)(2,1)}, bf16[4,128,1280]{2,1,0:T(8,128)(2,1)S(1)}, u32[]{:S(2)}) copy-start(bf16[4,128,1280]{2,1,0:T(8,128)(2,1)S(1)} %get-tuple-element.22) | copy-start | bytes 3932164
  43.3 32.4 %copy-start.19 = (bf16[256,128]{0,1:T(8,128)(2,1)}, bf16[256,128]{0,1:T(8,128)(2,1)S(1)}, u32[]{:S(2)}) copy-start(bf16[256,128]{0,1:T(8,128)(2,1)S(1)} %convolution_convert_fusion.5) | copy-start | bytes 196612
  44.0 32.3 %copy-start.21 = (bf16[256,128]{0,1:T(8,128)(2,1)}, bf16[256,128]{0,1:T(8,128)(2,1)S(1)}, u32[]{:S(2)}) copy-start(bf16[256,128]{0,1:T(8,128)(2,1)S(1)} %convolution_convert_fusion.6) | copy-start | bytes 196612
  44.3 31.9 %copy-start.23 = (bf16[256,128]{0,1:T(8,128)(2,1)}, bf16[256,128]{0,1:T(8,128)(2,1)S(1)}, u32[]{:S(2)}) copy-start(bf16[256,128]{0,1:T(8,128)(2,1)S(1)} %convolution_convert_fusion.4) | copy-start | bytes 196612
  67.3 31.7 %collective-permute-start.2 = (bf16[1024,640]{1,0:T(8,128)(2,1)}, bf16[1024,640]{1,0:T(8,128)(2,1)}, u32[]{:S(2)}, u32[]{:S(2)}) collective-permute-start(bf16[1024,640]{1,0:T(8,128)(2,1)} %all-gather.4.cloned.1.call-done), channel_id=1, source_target_pairs={{0,8},{8,0},{1,9},{9,1},{2,10},{10,2},{3,11},{11,3},{4,12},{12,4},... | collective-permute-start | bytes 3932168 | tf_op jit(solution)/shard_map/ppermute | solution.py:112
  75.7 1.4 copy-start.26
  77.1 21.9 %all-to-all-start.1 = ((bf16[8,256,128]{1,2,0:T(8,128)(2,1)}), bf16[8,256,128]{1,2,0:T(8,128)(2,1)S(1)}, u32[]{:S(2)}, u32[]{:S(2)}) async-start(bf16[8,256,128]{1,2,0:T(8,128)(2,1)} %broadcast_in_dim.34), calls=%async_computation.1 | async-start | bytes 1048576 | tf_op jit(solution)/shard_map/all_to_all | solution.py:104
  103.1 1.3 copy-start.4
  103.7 1.0 copy-start.1
  103.8 1.4 copy-start.10
  103.8 1.4 copy-start.12
  103.8 1.8 copy-start.11
  113.2 3.4 %copy-start.2 = (f32[256,1280]{1,0:T(8,128)S(1)}, f32[256,1280]{1,0:T(8,128)}, u32[]{:S(2)}) copy-start(f32[256,1280]{1,0:T(8,128)} %fusion.25) | copy-start | bytes 3932164
  118.8 23.3 %all-to-all-start.2 = ((bf16[8,32,1280]{2,1,0:T(8,128)(2,1)}), bf16[8,32,1280]{2,1,0:T(8,128)(2,1)}, u32[]{:S(2)}, u32[]{:S(2)}) async-start(bf16[8,32,1280]{2,1,0:T(8,128)(2,1)} %bitcast.176), calls=%async_computation.2 | async-start | bytes 1310720 | tf_op jit(solution)/shard_map/all_to_all | solution.py:210
  123.0 166.9 %all-gather.6.cloned.1.call-start = ((), (), s32[]{:S(2)}) async-start(), calls=%async_computation.7 | async-start | bytes 16220160 | tf_op jit(solution)/shard_map/all_gather | solution.py:212
  124.8 3.8 %collective-permute-start.3 = (bf16[384,640]{1,0:T(8,128)(2,1)S(1)}, bf16[384,640]{1,0:T(8,128)(2,1)S(1)}, u32[]{:S(2)}, u32[]{:S(2)}) collective-permute-start(bf16[384,640]{1,0:T(8,128)(2,1)S(1)} %select_convert_fusion.1), channel_id=1, source_target_pairs={{0,8},{8,0},{1,9},{9,1},{2,10},{10,2},{3,11},{11,3},{4,12},{12,4},... | collective-permute-start | bytes 1474568 | tf_op jit(solution)/shard_map/ppermute | solution.py:112
  144.2 22.4 %copy-start.20 = (bf16[256,128]{0,1:T(8,128)(2,1)S(1)}, bf16[256,128]{0,1:T(8,128)(2,1)}, u32[]{:S(2)}) copy-start(bf16[256,128]{0,1:T(8,128)(2,1)} %copy-done.19) | copy-start | bytes 196612
  144.2 22.4 %copy-start.22 = (bf16[256,128]{0,1:T(8,128)(2,1)S(1)}, bf16[256,128]{0,1:T(8,128)(2,1)}, u32[]{:S(2)}) copy-start(bf16[256,128]{0,1:T(8,128)(2,1)} %copy-done.21) | copy-start | bytes 196612
  144.2 22.4 %copy-start.27 = (f32[2,256]{1,0:T(2,128)S(1)}, f32[2,256]{1,0:T(2,128)}, u32[]{:S(2)}) copy-start(f32[2,256]{1,0:T(2,128)} %copy-done.26) | copy-start | bytes 6148
  166.5 1.5 copy-start.24
  166.5 1.5 copy-start.25
  170.8 6.6 %collective-permute-start.4 = (bf16[384,640]{1,0:T(8,128)(2,1)S(1)}, bf16[384,640]{1,0:T(8,128)(2,1)S(1)}, u32[]{:S(2)}, u32[]{:S(2)}) collective-permute-start(bf16[384,640]{1,0:T(8,128)(2,1)S(1)} %select_convert_fusion), channel_id=1, source_target_pairs={{0,8},{8,0},{1,9},{9,1},{2,10},{10,2},{3,11},{11,3},{4,12},{12,4},... | collective-permute-start | bytes 1474568 | tf_op jit(solution)/shard_map/ppermute | solution.py:112
  298.4 4.1 %collective-permute-start.5 = (bf16[384,640]{1,0:T(8,128)(2,1)S(1)}, bf16[384,640]{1,0:T(8,128)(2,1)S(1)}, u32[]{:S(2)}, u32[]{:S(2)}) collective-permute-start(bf16[384,640]{1,0:T(8,128)(2,1)S(1)} %broadcast_select_fusion.4), channel_id=1, source_target_pairs={{0,8},{8,0},{1,9},{9,1},{2,10},{10,2},{3,11},{11,3},{4,12},{12,4},... | collective-permute-start | bytes 1474568 | tf_op jit(solution)/shard_map/ppermute | solution.py:112
Sparse Core Ops, SparseCore 0:
  27.2 40.0 all-gather.3
  142.2 147.6 all-gather.5
